TPU v7x, 128 devices: a whole 4x4x4 slice. The times are simulated.
128 devices in a mesh: tm: 32 (over x, z, core), panel: 4 (over y).
Axes of the slice: x: 4, y: 4, z: 4, core: 2. Of those that a mesh axis runs over, the one named last changes fastest.
Arguments:
- design: bfloat16 [8192, 7680], P('tm', 'panel'), may hold values from -6 to 6
- partials: bfloat16 [8192, 64], P('tm'), may hold values from -0.119628906 to 0.119628906
- observed: bfloat16 [8192], P('tm'), may hold values from -6 to 6
- arc_of_row: int32 [8192, 1], replicated, may hold values from 0 to 31, as said below
- autoreg: float32 [32], replicated, may hold values from -0.55 to 0.5
- movavg: float32 [32], replicated, may hold values from 0.3 to 0.9
Outputs:
- normal: float32 [7680, 7680], P('tm', 'panel')
- right_hand: float32 [7680], P('panel')
Inputs may be any that keep to these rules, and one draw needn't show every extreme that they name: arc_of_row never falls along the epochs and names every arc; arcs 2b and 2b + 1 together have 2 * 256 epochs, one of them 384 // 3 to 160 epochs and the other 352 to 384; one arc has exactly 384 epochs and its partner exactly 128, so that at most 12 rows of one device belong to one arc, and every device holds exactly 12 rows of the longest arc; arc a is held by index a of tm.
All inputs are finite; a program needn't handle non-finite values.
Results may differ from a plain program's by a relative error of at most 0.02.
Values may be sent and summed in bfloat16 or wider, within the bound.
A program may use at most 192 MiB of HBM per device.

v0:
```python
import jax
import jax.numpy as jnp
from jax import lax
from jax.sharding import Mesh, PartitionSpec as P

TM = ("tmc", "core")


def whiten_matrix(order_row, order_col, usable_row, usable_col, ar_value, ma_value):
    spacing = order_row[:, None] - order_col[None, :]
    lag_steps = jnp.maximum(spacing - 1, 0)
    parity = (lag_steps % 2).astype(jnp.float32)
    flip_sign = 1.0 - 2.0 * parity
    decayed = (
        -(ar_value + ma_value)
        * flip_sign
        * jnp.exp(lag_steps.astype(jnp.float32) * jnp.log(ma_value))
    )
    entry = jnp.where(spacing == 0, jnp.float32(1.0), decayed)
    allowed = usable_row[:, None] & usable_col[None, :] & (spacing >= 0)
    return jnp.where(allowed, entry, jnp.float32(0.0)).astype(jnp.bfloat16)


def eliminate(whitener, rows_design, rows_params, rows_obs, scale):
    white_design = jnp.dot(whitener, rows_design, preferred_element_type=jnp.float32)
    white_params = jnp.dot(whitener, rows_params, preferred_element_type=jnp.float32)
    white_obs = jnp.dot(whitener, rows_obs, preferred_element_type=jnp.float32)
    param_count = rows_params.shape[1]
    param_gram = jnp.dot(white_params.T, white_params, precision=lax.Precision.HIGHEST) + jnp.eye(
        param_count, dtype=jnp.float32
    )
    factor = jnp.linalg.cholesky(param_gram)
    basis = lax.linalg.triangular_solve(factor, white_params.T, left_side=True, lower=True)
    arc_terms = jnp.dot(basis, white_design, precision=lax.Precision.HIGHEST)
    arc_rhs = jnp.dot(basis, white_obs, precision=lax.Precision.HIGHEST)
    right_part = (
        jnp.dot(white_design.T, white_obs, precision=lax.Precision.HIGHEST)
        - jnp.dot(arc_terms.T, arc_rhs, precision=lax.Precision.HIGHEST)
    ) * scale
    return (white_design.astype(jnp.bfloat16), basis, right_part)


def body(design, partials, observed, arc_of_row, autoreg, movavg):
    chip_count = lax.axis_size("tmc")
    core_count = lax.axis_size("core")
    core_index = lax.axis_index("core")
    tile_count = chip_count * core_count
    device_index = lax.axis_index("tmc") * core_count + core_index
    rows_dev = design.shape[0]
    panel_width = design.shape[1]
    param_count = partials.shape[1]
    capacity = 3 * rows_dev // 2 // tile_count
    slot_count = tile_count * capacity
    scale = 1.0 / (rows_dev * tile_count)
    arc_ids = arc_of_row[:, 0]
    epoch_table = arc_ids.reshape(rows_dev, tile_count)
    local_arcs = lax.dynamic_slice_in_dim(epoch_table, device_index, 1, 1)[:, 0]
    row_id = jnp.arange(rows_dev, dtype=jnp.int32)
    same_arc = local_arcs[:, None] == local_arcs[None, :]
    within = jnp.sum((same_arc & (row_id[None, :] < row_id[:, None])).astype(jnp.int32), axis=1)
    target_slot = local_arcs * capacity + within
    chooser = (target_slot[None, :] == jnp.arange(slot_count, dtype=jnp.int32)[:, None]).astype(
        jnp.bfloat16
    )

    def pick_rows(values):
        picked = jnp.dot(chooser, values, preferred_element_type=jnp.float32)
        return picked.astype(values.dtype)

    send_design = pick_rows(design).reshape(tile_count, capacity, panel_width)
    with_obs = jnp.concatenate([partials, observed[:, None]], axis=1)
    send_params = pick_rows(with_obs).reshape(tile_count, capacity, param_count + 1)
    got_params = lax.all_to_all(send_params, TM, split_axis=0, concat_axis=0, tiled=True)
    send_design, got_params = lax.optimization_barrier((send_design, got_params))
    got_design = lax.all_to_all(send_design, TM, split_axis=0, concat_axis=0, tiled=True)
    got_design = got_design.reshape(slot_count, panel_width)
    got_params = got_params.reshape(slot_count, param_count + 1)
    got_obs = got_params[:, param_count]
    got_params = got_params[:, :param_count]
    per_source = jnp.sum((epoch_table == device_index).astype(jnp.int32), axis=0)
    arc_start = jnp.sum((arc_ids < device_index).astype(jnp.int32))
    first_pos = jnp.mod(jnp.arange(tile_count, dtype=jnp.int32) - arc_start, tile_count)
    offset_in = jnp.arange(capacity, dtype=jnp.int32)
    order_pos = (first_pos[:, None] + offset_in[None, :] * tile_count).reshape(slot_count)
    usable = (offset_in[None, :] < per_source[:, None]).reshape(slot_count)
    position = jnp.arange(slot_count, dtype=jnp.int32)
    arc_length = jnp.sum(per_source)
    whitener = whiten_matrix(
        position,
        order_pos,
        position < arc_length,
        usable,
        autoreg[device_index],
        movavg[device_index],
    )
    design_bf, basis, right_part = eliminate(whitener, got_design, got_params, got_obs, scale)
    swap = [(0, 1), (1, 0)]
    short_most = 5 * rows_dev // 8
    keep = (slot_count + short_most) // 2
    moved = lax.ppermute(design_bf[keep:], "core", swap)
    packed = design_bf[:keep].at[short_most : short_most + moved.shape[0]].add(moved)
    got_basis = lax.ppermute(basis, "core", swap)
    packed, right_part, got_basis = lax.optimization_barrier((packed, right_part, got_basis))
    gathered = lax.all_gather(packed, "panel", axis=1, tiled=True)
    right_hand = lax.psum(right_part + lax.ppermute(right_part, "core", swap), "tmc")
    gathered, right_hand = lax.optimization_barrier((gathered, right_hand))
    half = panel_width // core_count
    got_rows = lax.ppermute(gathered, "core", swap)
    moved_count = slot_count - keep

    def spread(own_basis):
        lead = own_basis[:, :keep]
        tail = jnp.pad(own_basis[:, keep:], ((0, 0), (short_most, keep - short_most - moved_count)))
        return (lead, tail)

    own_lead, own_tail = spread(basis)
    far_lead, far_tail = spread(got_basis)
    stacked_basis = jnp.concatenate(
        [
            jnp.concatenate([own_lead, own_tail], axis=1),
            jnp.concatenate([far_tail, far_lead], axis=1),
        ],
        axis=0,
    ).astype(jnp.bfloat16)
    design_side = jnp.concatenate([gathered, got_rows], axis=0)
    own_share = jnp.dot(stacked_basis[:, :keep], gathered, preferred_element_type=jnp.float32)
    far_share = jnp.dot(stacked_basis[:, keep:], got_rows, preferred_element_type=jnp.float32)
    terms = (own_share + far_share).astype(jnp.bfloat16)
    row_side = jnp.concatenate([design_side, -terms], axis=0)
    col_side = lax.dynamic_slice_in_dim(
        jnp.concatenate([design_side, terms], axis=0),
        lax.axis_index("panel") * panel_width + core_index * half,
        half,
        1,
    )
    product = lax.dot_general(
        row_side, col_side, (((0,), (0,)), ((), ())), preferred_element_type=jnp.float32
    )
    pair = lax.psum_scatter(
        (product * scale).astype(jnp.bfloat16), "tmc", scatter_dimension=0, tiled=True
    )
    block_rows = pair.shape[0] // core_count
    by_core = pair.reshape(core_count, block_rows, half)
    mine = jnp.where(core_index == 0, by_core[0], by_core[1])
    given = jnp.where(core_index == 0, by_core[1], by_core[0])
    got = lax.ppermute(given, "core", swap)
    first = jnp.where(core_index == 0, mine, got)
    second = jnp.where(core_index == 0, got, mine)
    normal = jnp.concatenate([first, second], axis=1).astype(jnp.float32)
    return (normal, right_hand)


def solution(mesh):
    chips = mesh.devices.shape[0] // 2
    split = Mesh(mesh.devices.reshape(chips, 2, mesh.devices.shape[1]), ("tmc", "core", "panel"))
    in_specs = (P(TM, "panel"), P(TM, None), P(TM), P(), P(), P())
    out_specs = (P(TM, "panel"), P("panel"))
    return jax.shard_map(body, mesh=split, in_specs=in_specs, out_specs=out_specs, check_vma=False)
```

profile of v0, /device:TPU:1, one launch (start us, length us, event | category | flops | bytes accessed | tf_op | source)
XLA Modules:
  0.0 268.0 jit_solution(4440556200000650307)
XLA Ops:
  7.2 0.7 broadcast_in_dim.12
  8.5 2.3 fusion.53
  11.2 1.0 convolution_convert_fusion.1
  12.3 0.8 reshape.152
  13.1 9.4 %all-to-all-start = ((bf16[32,2,390]{2,1,0:T(2,128)(2,1)}), bf16[32,2,390]{2,1,0:T(2,128)(2,1)S(1)}, u32[]{:S(2)}, u32[]{:S(2)}) async-start(bf16[32,2,390]{2,1,0:T(2,128)(2,1)} %reshape.152), calls=%async_computation | async-start | bytes 131072 | tf_op jit(solution)/shard_map/all_to_all | solution.py:73
  22.6 0.7 and_select_fusion
  28.3 1.5 reshape.124
  30.1 7.2 %all-to-all-start.1 = ((bf16[32,12,1920]{2,1,0:T(8,128)(2,1)}), bf16[32,12,1920]{2,1,0:T(8,128)(2,1)S(1)}, u32[]{:S(2)}, u32[]{:S(2)}) async-start(bf16[32,12,1920]{2,1,0:T(8,128)(2,1)} %reshape.124), calls=%async_computation.1 | async-start | bytes 3932160 | tf_op jit(solution)/shard_map/all_to_all | solution.py:75
  37.4 0.7 fusion.34
  38.6 5.8 %cholesky.17 = f32[64,64]{1,0:T(8,128)S(1)} custom-call(f32[64,64]{1,0:T(8,128)S(1)} %fusion.58), custom_call_target="Cholesky" | custom-call | tf_op jit(solution)/shard_map/jit(cholesky)/cholesky | solution.py:32
  45.8 4.9 %custom-call.6 = f32[1,64,64]{1,2,0:T(8,128)S(1)} custom-call(f32[1,64,64]{2,1,0:T(8,128)S(1)} %fusion.52), custom_call_target="InvertDiagBlocksLowerTriangular" | custom-call | tf_op jit(solution)/shard_map/triangular_solve | solution.py:33
  52.2 12.0 %all-to-all-done.1 = bf16[32,12,1920]{2,1,0:T(8,128)(2,1)S(1)} async-done(((bf16[32,12,1920]{2,1,0:T(8,128)(2,1)}), bf16[32,12,1920]{2,1,0:T(8,128)(2,1)S(1)}, u32[]{:S(2)}, u32[]{:S(2)}) %all-to-all-start.1) | async-done | bytes 1474592 | tf_op jit(solution)/shard_map/all_to_all | solution.py:75
  64.2 1.3 reshape.126
  65.5 2.8 %fusion.85 = (bf16[384,1920]{1,0:T(8,128)(2,1)S(1)}, f32[384,1920]{1,0:T(8,128)S(1)}) fusion(bf16[384,1920]{1,0:T(8,128)(2,1)} %reshape.126, f32[]{:T(128)} %bitcast.1, f32[]{:T(128)} %bitcast, s32[384]{0:T(512)S(1)} %add.105, pred[384]{0:T(512)(128)(4,1)S(1)} %lt.73, pred[384]{0:T(512)(128)(4,1)S(1)} %iota_compare_fusion.12), kind=kOutput, calls=%fused_computation.126 | convolution fusion | flops 570359808 | bytes 5900552 | tf_op jit(solution)/shard_map/dot_general | solution.py:25
  68.4 1.8 fusion.88
  70.2 1.1 collective-permute-start
  71.7 1.7 fusion.9
  73.6 0.9 copy-done.2
  74.7 1.2 collective-permute-done.2
  75.8 30.8 %psum.7 = f32[1920]{0:T(1024)} all-reduce(f32[1920]{0:T(1024)S(1)} %add.114), channel_id=1, replica_groups=mesh['tmc'=16,'core'=2,'panel'=4] {'tmc'}, use_global_device_ids=true, to_apply=%region_6.7 | all-reduce | flops 1920 | bytes 15360 | tf_op jit(solution)/shard_map/psum | solution.py:105
  106.6 13.1 %all-gather.2.cloned.1.call-done = bf16[272,7680]{1,0:T(8,128)(2,1)} async-done(((bf16[272,1920]{1,0:T(8,128)(2,1)}), bf16[272,7680]{1,0:T(8,128)(2,1)}) %all-gather.2.cloned.1.call-update) | async-done | bytes 4177936 | tf_op jit(solution)/shard_map/all_gather | solution.py:104
  119.7 0.7 collective-permute-start.3
  120.7 3.4 %fusion.46 = f32[128,7680]{1,0:T(8,128)S(1)} fusion(bf16[272,7680]{1,0:T(8,128)(2,1)} %all-gather.2.cloned.1.call-done, bf16[128,544]{1,0:T(8,128)(2,1)S(1)} %fusion.43), kind=kOutput, calls=%fused_computation.70 | convolution fusion | flops 534773760 | bytes 8208384 | tf_op jit(solution)/shard_map/dot_general | solution.py:126
  124.1 3.5 %collective-permute-done.3 = bf16[272,7680]{1,0:T(8,128)(2,1)} collective-permute-done((bf16[272,7680]{1,0:T(8,128)(2,1)}, bf16[272,7680]{1,0:T(8,128)(2,1)}, u32[]{:S(2)}, u32[]{:S(2)}) %collective-permute-start.3) | collective-permute-done | bytes 4177952 | tf_op jit(solution)/shard_map/ppermute | solution.py:108
  127.6 3.4 %fusion.86 = (bf16[128,7680]{1,0:T(8,128)(2,1)S(1)}, bf16[128,7680]{1,0:T(8,128)(2,1)S(1)}) fusion(f32[128,7680]{1,0:T(8,128)S(1)} %fusion.46, bf16[272,7680]{1,0:T(8,128)(2,1)} %collective-permute-done.3, bf16[128,544]{1,0:T(8,128)(2,1)S(1)} %fusion.43), kind=kOutput, calls=%fused_computation.127 | convolution fusion | flops 537722880 | bytes 12140544 | tf_op jit(solution)/shard_map/dot_general | solution.py:127
  131.0 18.2 %multiply_convert_fusion = bf16[7680,960]{1,0:T(8,128)(2,1)} fusion(bf16[272,7680]{1,0:T(8,128)(2,1)} %collective-permute-done.3, bf16[272,7680]{1,0:T(8,128)(2,1)S(1)} %copy-done.1, bf16[128,7680]{1,0:T(8,128)(2,1)S(1)} %get-tuple-element.38, s32[]{:T(128)S(6)} %select_n.64, bf16[128,7680]{1,0:T(8,128)(2,1)S(1)} %get-tuple-element.39), kind=kOutput, calls=%fused_computation | convolution fusion | flops 9958625280 | bytes 35389444 | tf_op jit(solution)/shard_map/dot_general | solution.py:136
  149.2 105.4 %reduce-scatter.2.cloned.1.call-done = bf16[480,960]{1,0:T(8,128)(2,1)} async-done(((bf16[7680,960]{1,0:T(8,128)(2,1)}), bf16[480,960]{1,0:T(8,128)(2,1)}) %reduce-scatter.2.cloned.1.call-update) | async-done | bytes 921616 | tf_op jit(solution)/shard_map/reduce_scatter | solution.py:139
  254.6 1.2 broadcast_select_fusion.2
  255.8 1.1 collective-permute-start.4
  256.9 1.5 collective-permute-done.4
  258.4 1.3 broadcast_select_fusion.1
  259.7 1.5 maximum_convert_fusion
  (57 shorter events, 8.9 us)
Async XLA Ops:
  7.2 16.3 %copy-start = (bf16[256,1920]{1,0:T(8,128)(2,1)S(1)}, bf16[256,1920]{1,0:T(8,128)(2,1)}, u32[]{:S(2)}) copy-start(bf16[256,1920]{1,0:T(8,128)(2,1)} %param.8) | copy-start | bytes 2949124
  7.2 17.6 %copy-start.3 = (f32[32]{0:T(128)S(1)}, f32[32]{0:T(128)}, u32[]{:S(2)}) copy-start(f32[32]{0:T(128)} %param.13) | copy-start | bytes 388
  7.2 18.8 %copy-start.4 = (f32[32]{0:T(128)S(1)}, f32[32]{0:T(128)}, u32[]{:S(2)}) copy-start(f32[32]{0:T(128)} %param.12) | copy-start | bytes 388
  13.1 16.8 %all-to-all-start = ((bf16[32,2,390]{2,1,0:T(2,128)(2,1)}), bf16[32,2,390]{2,1,0:T(2,128)(2,1)S(1)}, u32[]{:S(2)}, u32[]{:S(2)}) async-start(bf16[32,2,390]{2,1,0:T(2,128)(2,1)} %reshape.152), calls=%async_computation | async-start | bytes 131072 | tf_op jit(solution)/shard_map/all_to_all | solution.py:73
  30.1 34.1 %all-to-all-start.1 = ((bf16[32,12,1920]{2,1,0:T(8,128)(2,1)}), bf16[32,12,1920]{2,1,0:T(8,128)(2,1)S(1)}, u32[]{:S(2)}, u32[]{:S(2)}) async-start(bf16[32,12,1920]{2,1,0:T(8,128)(2,1)} %reshape.124), calls=%async_computation.1 | async-start | bytes 3932160 | tf_op jit(solution)/shard_map/all_to_all | solution.py:75
  37.3 82.4 %all-gather.2.cloned.1.call-start = ((), (), s32[]{:S(2)}) async-start(), calls=%async_computation.3 | async-start | bytes 5222400 | tf_op jit(solution)/shard_map/all_gather | solution.py:104
  51.0 22.5 %collective-permute-start.1 = (bf16[64,384]{1,0:T(8,128)(2,1)S(1)}, bf16[64,384]{1,0:T(8,128)(2,1)S(1)}, u32[]{:S(2)}, u32[]{:S(2)}) collective-permute-start(bf16[64,384]{1,0:T(8,128)(2,1)S(1)} %get-tuple-element.33), channel_id=1, source_target_pairs={{0,4},{4,0},{1,5},{5,1},{2,6},{6,2},{3,7},{7,3},{8,12},{12,8},{9,1... | collective-permute-start | bytes 147464 | tf_op jit(solution)/shard_map/ppermute | solution.py:102
  70.2 3.2 %collective-permute-start = (bf16[112,1920]{1,0:T(8,128)(2,1)S(1)}, bf16[112,1920]{1,0:T(8,128)(2,1)S(1)}, u32[]{:S(2)}, u32[]{:S(2)}) collective-permute-start(bf16[112,1920]{1,0:T(8,128)(2,1)S(1)} %slice.89), channel_id=1, source_target_pairs={{0,4},{4,0},{1,5},{5,1},{2,6},{6,2},{3,7},{7,3},{8,12},{12,8},{9,1... | collective-permute-start | bytes 1290248 | tf_op jit(solution)/shard_map/ppermute | solution.py:100
  73.5 1.0 copy-start.2
  74.5 180.1 %reduce-scatter.2.cloned.1.call-start = ((), (), s32[]{:S(2)}) async-start(), calls=%async_computation.4 | async-start | bytes 16711680 | tf_op jit(solution)/shard_map/reduce_scatter | solution.py:139
  74.6 1.3 collective-permute-start.2
  119.7 7.8 %collective-permute-start.3 = (bf16[272,7680]{1,0:T(8,128)(2,1)}, bf16[272,7680]{1,0:T(8,128)(2,1)}, u32[]{:S(2)}, u32[]{:S(2)}) collective-permute-start(bf16[272,7680]{1,0:T(8,128)(2,1)} %all-gather.2.cloned.1.call-done), channel_id=1, source_target_pairs={{0,4},{4,0},{1,5},{5,1},{2,6},{6,2},{3,7},{7,3},{8,12},{12,8},{9,1... | collective-permute-start | bytes 12533768 | tf_op jit(solution)/shard_map/ppermute | solution.py:108
  124.1 6.9 %copy-start.1 = (bf16[272,7680]{1,0:T(8,128)(2,1)S(1)}, bf16[272,7680]{1,0:T(8,128)(2,1)}, u32[]{:S(2)}) copy-start(bf16[272,7680]{1,0:T(8,128)(2,1)} %all-gather.2.cloned.1.call-done) | copy-start | bytes 12533764
  255.8 2.6 collective-permute-start.4
Sparse Core Ops, SparseCore 0:
  74.6 45.0 all-gather.1
  149.3 105.1 reduce-scatter.1
where the time goes:
time: 269 us; the launch traced here: 268 us
  waiting for transfers between devices  137 us (51%)
  matrix products  35.2 us (13%)
  blocking collectives  30.8 us (11%)
  other arithmetic  20.3 us (8%)
  starting transfers between devices  20 us (7%)
  between operations  16.4 us (6%)
  local copies, waits for them, and re-layouts  8.41 us (3%)
    reduce_scatter x1, waiting for transfers between devices, body(): lax.psum_scatter((product * scale).astype(jnp.bfloat16), 'tmc', scatter_d...  105 us
    psum x1, blocking collectives, body(): lax.psum(right_part + lax.ppermute(right_part, 'core', swap), 'tmc')  30.8 us
    dot_general x1, matrix products, body(): lax.dot_general(row_side, col_side, (((0,), (0,)), ((), ())), preferred_e...  18.2 us
    all_gather x1, waiting for transfers between devices, body(): gathered = lax.all_gather(packed, 'panel', axis=1, tiled=True)  13.1 us
    all_to_all x1, waiting for transfers between devices, body(): lax.all_to_all(send_design, TM, split_axis=0, concat_axis=0, tiled=True)  12 us
    all_to_all x1, starting transfers between devices, body(): lax.all_to_all(send_params, TM, split_axis=0, concat_axis=0, tiled=True)  9.43 us
    all_to_all x1, starting transfers between devices, body(): lax.all_to_all(send_design, TM, split_axis=0, concat_axis=0, tiled=True)  7.18 us
    another operation x3, other arithmetic, eliminate(): factor = jnp.linalg.cholesky(param_gram)  6.52 us
  transfers between devices with their start and end apart: 9, of which 7 were waited for; matrix products, arithmetic and copies ran while one was open for 12% of the time, Pallas kernels for 0%

commit v1 on v0

--- a/solution.py
+++ b/solution.py
@@ -101,7 +101,8 @@
     packed = design_bf[:keep].at[short_most : short_most + moved.shape[0]].add(moved)
     got_basis = lax.ppermute(basis, "core", swap)
     packed, right_part, got_basis = lax.optimization_barrier((packed, right_part, got_basis))
-    gathered = lax.all_gather(packed, "panel", axis=1, tiled=True)
+    outgoing = jnp.stack([packed] * lax.axis_size("panel"))
+    gathered = jnp.concatenate(lax.all_to_all(outgoing, "panel", 0, 0), axis=1)
     right_hand = lax.psum(right_part + lax.ppermute(right_part, "core", swap), "tmc")
     gathered, right_hand = lax.optimization_barrier((gathered, right_hand))
     half = panel_width // core_count

time: 269 us -> 279 us (1.037)
  local copies, waits for them, and re-layouts: 8.41 us -> 14.2 us
  starting transfers between devices: 20 us -> 24.8 us
    all_to_all x0 -> x1, waiting for transfers between devices: none -> 16.8 us  [body(): gathered = jnp.concatenate(lax.all_to_all(outgoing, 'panel', 0, 0), axis=1)]
    all_gather x1 -> x0, waiting for transfers between devices: 13.1 us -> none  [body(): gathered = lax.all_gather(packed, 'panel', axis=1, tiled=True)]
    all_to_all x0 -> x1, starting transfers between devices: none -> 4.86 us  [body(): gathered = jnp.concatenate(lax.all_to_all(outgoing, 'panel', 0, 0), axis=1)]
    reduce_scatter x1, waiting for transfers between devices: 105 us -> 101 us  [body(): lax.psum_scatter((product * scale).astype(jnp.bfloat16), 'tmc', scatter_d...]
    reshape x0 -> x1, local copies, waits for them, and re-layouts: none -> 4.51 us  [body(): gathered = jnp.concatenate(lax.all_to_all(outgoing, 'panel', 0, 0), axis=1)]
  transfers between devices with their start and end apart: 9 -> 9, of which waited for: 7 -> 7; matrix products, arithmetic and copies ran while one was open for 12% -> 11% of each run, Pallas kernels for 0% -> 0%
where the time goes in v1:
time: 279 us; the launch traced here: 278 us
  waiting for transfers between devices  136 us (49%)
  matrix products  36 us (13%)
  blocking collectives  30.8 us (11%)
  starting transfers between devices  24.8 us (9%)
  other arithmetic  20.3 us (7%)
  between operations  16.4 us (6%)
  local copies, waits for them, and re-layouts  14.2 us (5%)
    reduce_scatter x1, waiting for transfers between devices, body(): lax.psum_scatter((product * scale).astype(jnp.bfloat16), 'tmc', scatter_d...  101 us
    psum x1, blocking collectives, body(): lax.psum(right_part + lax.ppermute(right_part, 'core', swap), 'tmc')  30.8 us
    dot_general x1, matrix products, body(): lax.dot_general(row_side, col_side, (((0,), (0,)), ((), ())), preferred_e...  18.9 us
    all_to_all x1, waiting for transfers between devices, body(): gathered = jnp.concatenate(lax.all_to_all(outgoing, 'panel', 0, 0), axis=1)  16.8 us
    all_to_all x1, waiting for transfers between devices, body(): lax.all_to_all(send_design, TM, split_axis=0, concat_axis=0, tiled=True)  12.1 us
    all_to_all x1, starting transfers between devices, body(): lax.all_to_all(send_params, TM, split_axis=0, concat_axis=0, tiled=True)  9.43 us
    all_to_all x1, starting transfers between devices, body(): lax.all_to_all(send_design, TM, split_axis=0, concat_axis=0, tiled=True)  7.18 us
    another operation x3, other arithmetic, eliminate(): factor = jnp.linalg.cholesky(param_gram)  6.52 us
  transfers between devices with their start and end apart: 9, of which 7 were waited for; matrix products, arithmetic and copies ran while one was open for 11% of the time, Pallas kernels for 0%

profile of v1, /device:TPU:1, one launch (start us, length us, event | category | flops | bytes accessed | tf_op | source)
XLA Modules:
  0.0 278.3 jit_solution(612884135441769149)
XLA Ops:
  7.2 0.7 broadcast_in_dim.12
  8.5 2.3 fusion.53
  11.2 1.0 convolution_convert_fusion.1
  12.3 0.8 reshape.162
  13.1 9.4 %all-to-all-start = ((bf16[32,2,390]{2,1,0:T(2,128)(2,1)}), bf16[32,2,390]{2,1,0:T(2,128)(2,1)S(1)}, u32[]{:S(2)}, u32[]{:S(2)}) async-start(bf16[32,2,390]{2,1,0:T(2,128)(2,1)} %reshape.162), calls=%async_computation | async-start | bytes 131072 | tf_op jit(solution)/shard_map/all_to_all | solution.py:73
  28.3 1.5 reshape.132
  30.1 7.2 %all-to-all-start.1 = ((bf16[32,12,1920]{2,1,0:T(8,128)(2,1)}), bf16[32,12,1920]{2,1,0:T(8,128)(2,1)S(1)}, u32[]{:S(2)}, u32[]{:S(2)}) async-start(bf16[32,12,1920]{2,1,0:T(8,128)(2,1)} %reshape.132), calls=%async_computation.1 | async-start | bytes 3932160 | tf_op jit(solution)/shard_map/all_to_all | solution.py:75
  38.6 5.8 %cholesky.17 = f32[64,64]{1,0:T(8,128)S(1)} custom-call(f32[64,64]{1,0:T(8,128)S(1)} %fusion.58), custom_call_target="Cholesky" | custom-call | tf_op jit(solution)/shard_map/jit(cholesky)/cholesky | solution.py:32
  45.8 4.9 %custom-call.6 = f32[1,64,64]{1,2,0:T(8,128)S(1)} custom-call(f32[1,64,64]{2,1,0:T(8,128)S(1)} %fusion.52), custom_call_target="InvertDiagBlocksLowerTriangular" | custom-call | tf_op jit(solution)/shard_map/triangular_solve | solution.py:33
  52.1 12.1 %all-to-all-done.1 = bf16[32,12,1920]{2,1,0:T(8,128)(2,1)S(1)} async-done(((bf16[32,12,1920]{2,1,0:T(8,128)(2,1)}), bf16[32,12,1920]{2,1,0:T(8,128)(2,1)S(1)}, u32[]{:S(2)}, u32[]{:S(2)}) %all-to-all-start.1) | async-done | bytes 1474592 | tf_op jit(solution)/shard_map/all_to_all | solution.py:75
  64.2 1.3 reshape.134
  65.5 2.8 fusion.85
  68.4 1.8 fusion.88
  70.2 1.1 collective-permute-start
  71.7 1.7 fusion.9
  73.5 2.2 stack.2
  75.8 4.9 %all-to-all-start.2 = ((bf16[4,272,1920]{2,1,0:T(8,128)(2,1)}), bf16[4,272,1920]{2,1,0:T(8,128)(2,1)}, u32[]{:S(2)}, u32[]{:S(2)}) async-start(bf16[4,272,1920]{2,1,0:T(8,128)(2,1)} %stack.2), calls=%async_computation.2 | async-start | bytes 8355840 | tf_op jit(solution)/shard_map/all_to_all | solution.py:105
  80.8 1.2 collective-permute-done.2
  82.0 30.8 %psum.7 = f32[1920]{0:T(1024)} all-reduce(f32[1920]{0:T(1024)S(1)} %add.114), channel_id=1, replica_groups=mesh['tmc'=16,'core'=2,'panel'=4] {'tmc'}, use_global_device_ids=true, to_apply=%region_6.7 | all-reduce | flops 1920 | bytes 15360 | tf_op jit(solution)/shard_map/psum | solution.py:106
  112.7 16.8 %all-to-all-done.2 = bf16[4,272,1920]{2,1,0:T(8,128)(2,1)} async-done(((bf16[4,272,1920]{2,1,0:T(8,128)(2,1)}), bf16[4,272,1920]{2,1,0:T(8,128)(2,1)}, u32[]{:S(2)}, u32[]{:S(2)}) %all-to-all-start.2) | async-done | bytes 4177952 | tf_op jit(solution)/shard_map/all_to_all | solution.py:105
  129.5 4.5 %copy.19 = bf16[4,34,8,1920]{3,2,0,1:T(8,128)(2,1)} copy(bf16[4,34,8,1920]{3,2,1,0:T(8,128)(2,1)} %bitcast.10) | data formatting | bytes 8355840 | tf_op jit(solution)/shard_map/reshape | solution.py:105
  134.0 0.8 collective-permute-start.3
  135.1 3.4 %fusion.46 = f32[128,7680]{1,0:T(8,128)S(1)} fusion(bf16[272,7680]{1,0:T(8,128)(2,1)} %bitcast.11, bf16[128,544]{1,0:T(8,128)(2,1)S(1)} %fusion.43), kind=kOutput, calls=%fused_computation.70 | convolution fusion | flops 534773760 | bytes 8208384 | tf_op jit(solution)/shard_map/dot_general | solution.py:127
  138.4 3.5 %collective-permute-done.3 = bf16[272,7680]{1,0:T(8,128)(2,1)} collective-permute-done((bf16[272,7680]{1,0:T(8,128)(2,1)}, bf16[272,7680]{1,0:T(8,128)(2,1)}, u32[]{:S(2)}, u32[]{:S(2)}) %collective-permute-start.3) | collective-permute-done | bytes 4177952 | tf_op jit(solution)/shard_map/ppermute | solution.py:109
  141.9 3.4 %fusion.86 = (bf16[128,7680]{1,0:T(8,128)(2,1)S(1)}, bf16[128,7680]{1,0:T(8,128)(2,1)S(1)}) fusion(f32[128,7680]{1,0:T(8,128)S(1)} %fusion.46, bf16[272,7680]{1,0:T(8,128)(2,1)} %collective-permute-done.3, bf16[128,544]{1,0:T(8,128)(2,1)S(1)} %fusion.43), kind=kOutput, calls=%fused_computation.127 | convolution fusion | flops 537722880 | bytes 12140544 | tf_op jit(solution)/shard_map/dot_general | solution.py:128
  145.3 18.9 %multiply_convert_fusion = bf16[7680,960]{1,0:T(8,128)(2,1)} fusion(bf16[272,7680]{1,0:T(8,128)(2,1)} %collective-permute-done.3, bf16[272,7680]{1,0:T(8,128)(2,1)} %bitcast.11, bf16[128,7680]{1,0:T(8,128)(2,1)S(1)} %get-tuple-element.38, s32[]{:T(128)S(6)} %select_n.64, bf16[128,7680]{1,0:T(8,128)(2,1)S(1)} %get-tuple-element.39), kind=kOutput, calls=%fused_computation | convolution fusion | flops 9958625280 | bytes 35389444 | tf_op jit(solution)/shard_map/dot_general | solution.py:137
  164.3 100.7 %reduce-scatter.2.cloned.1.call-done = bf16[480,960]{1,0:T(8,128)(2,1)} async-done(((bf16[7680,960]{1,0:T(8,128)(2,1)}), bf16[480,960]{1,0:T(8,128)(2,1)}) %reduce-scatter.2.cloned.1.call-update) | async-done | bytes 921616 | tf_op jit(solution)/shard_map/reduce_scatter | solution.py:140
  265.0 1.2 broadcast_select_fusion.2
  266.2 1.0 collective-permute-start.4
  267.3 1.5 collective-permute-done.4
  268.7 1.3 broadcast_select_fusion.1
  270.0 1.5 maximum_convert_fusion
  (54 shorter events, 10.2 us)
Async XLA Ops:
  7.2 16.3 %copy-start = (bf16[256,1920]{1,0:T(8,128)(2,1)S(1)}, bf16[256,1920]{1,0:T(8,128)(2,1)}, u32[]{:S(2)}) copy-start(bf16[256,1920]{1,0:T(8,128)(2,1)} %param.8) | copy-start | bytes 2949124
  7.2 17.6 %copy-start.1 = (f32[32]{0:T(128)S(1)}, f32[32]{0:T(128)}, u32[]{:S(2)}) copy-start(f32[32]{0:T(128)} %param.13) | copy-start | bytes 388
  7.2 18.8 %copy-start.2 = (f32[32]{0:T(128)S(1)}, f32[32]{0:T(128)}, u32[]{:S(2)}) copy-start(f32[32]{0:T(128)} %param.12) | copy-start | bytes 388
  13.1 16.8 %all-to-all-start = ((bf16[32,2,390]{2,1,0:T(2,128)(2,1)}), bf16[32,2,390]{2,1,0:T(2,128)(2,1)S(1)}, u32[]{:S(2)}, u32[]{:S(2)}) async-start(bf16[32,2,390]{2,1,0:T(2,128)(2,1)} %reshape.162), calls=%async_computation | async-start | bytes 131072 | tf_op jit(solution)/shard_map/all_to_all | solution.py:73
  30.1 34.1 %all-to-all-start.1 = ((bf16[32,12,1920]{2,1,0:T(8,128)(2,1)}), bf16[32,12,1920]{2,1,0:T(8,128)(2,1)S(1)}, u32[]{:S(2)}, u32[]{:S(2)}) async-start(bf16[32,12,1920]{2,1,0:T(8,128)(2,1)} %reshape.132), calls=%async_computation.1 | async-start | bytes 3932160 | tf_op jit(solution)/shard_map/all_to_all | solution.py:75
  51.0 22.5 %collective-permute-start.1 = (bf16[64,384]{1,0:T(8,128)(2,1)S(1)}, bf16[64,384]{1,0:T(8,128)(2,1)S(1)}, u32[]{:S(2)}, u32[]{:S(2)}) collective-permute-start(bf16[64,384]{1,0:T(8,128)(2,1)S(1)} %get-tuple-element.33), channel_id=1, source_target_pairs={{0,4},{4,0},{1,5},{5,1},{2,6},{6,2},{3,7},{7,3},{8,12},{12,8},{9,1... | collective-permute-start | bytes 147464 | tf_op jit(solution)/shard_map/ppermute | solution.py:102
  70.2 3.2 %collective-permute-start = (bf16[112,1920]{1,0:T(8,128)(2,1)S(1)}, bf16[112,1920]{1,0:T(8,128)(2,1)S(1)}, u32[]{:S(2)}, u32[]{:S(2)}) collective-permute-start(bf16[112,1920]{1,0:T(8,128)(2,1)S(1)} %slice.89), channel_id=1, source_target_pairs={{0,4},{4,0},{1,5},{5,1},{2,6},{6,2},{3,7},{7,3},{8,12},{12,8},{9,1... | collective-permute-start | bytes 1290248 | tf_op jit(solution)/shard_map/ppermute | solution.py:100
  75.8 53.7 %all-to-all-start.2 = ((bf16[4,272,1920]{2,1,0:T(8,128)(2,1)}), bf16[4,272,1920]{2,1,0:T(8,128)(2,1)}, u32[]{:S(2)}, u32[]{:S(2)}) async-start(bf16[4,272,1920]{2,1,0:T(8,128)(2,1)} %stack.2), calls=%async_computation.2 | async-start | bytes 8355840 | tf_op jit(solution)/shard_map/all_to_all | solution.py:105
  80.7 184.3 %reduce-scatter.2.cloned.1.call-start = ((), (), s32[]{:S(2)}) async-start(), calls=%async_computation.4 | async-start | bytes 16711680 | tf_op jit(solution)/shard_map/reduce_scatter | solution.py:140
  80.7 1.3 collective-permute-start.2
  134.0 7.9 %collective-permute-start.3 = (bf16[272,7680]{1,0:T(8,128)(2,1)}, bf16[272,7680]{1,0:T(8,128)(2,1)}, u32[]{:S(2)}, u32[]{:S(2)}) collective-permute-start(bf16[272,7680]{1,0:T(8,128)(2,1)} %bitcast.11), channel_id=1, source_target_pairs={{0,4},{4,0},{1,5},{5,1},{2,6},{6,2},{3,7},{7,3},{8,12},{12,8},{9,1... | collective-permute-start | bytes 12533768 | tf_op jit(solution)/shard_map/ppermute | solution.py:109
  266.2 2.5 collective-permute-start.4
Sparse Core Ops, SparseCore 0:
  164.4 100.5 reduce-scatter.1
